TPU v7x, 256 devices: a whole 4x4x8 slice. The times are simulated.
256 devices in a mesh: row: 32 (over z_lo, x, core), col: 8 (over z_hi, y).
Axes of the slice: x: 4, y: 4, z: 8 (z_hi: 2, z_lo: 4; z = z_hi * 4 + z_lo), core: 2. Of those that a mesh axis runs over, the one named last changes fastest.
Arguments:
- pair: bfloat16 [512, 512, 128], P('row', 'col'), may hold values from -6 to 6
- cotangent: bfloat16 [64, 512, 512], P(None, 'row', 'col'), may hold values from -0.59765625 to 0.59765625
- w_left: bfloat16 [128, 64], replicated, may hold values from -0.5 to 0.5
- w_left_gate: bfloat16 [128, 64], replicated, may hold values from -0.5 to 0.5
- w_right: bfloat16 [128, 64], replicated, may hold values from -0.5 to 0.5
- w_right_gate: bfloat16 [128, 64], replicated, may hold values from -0.5 to 0.5
Outputs:
- pair_gradient: bfloat16 [512, 512, 128], P('row', 'col')
- grad_left: float32 [128, 64], replicated
- grad_left_gate: float32 [128, 64], replicated
- grad_right: float32 [128, 64], replicated
- grad_right_gate: float32 [128, 64], replicated
All inputs are finite; a program needn't handle non-finite values.
Results may differ from a plain program's by a relative error of at most 0.0082.
Values may be sent and summed in bfloat16 or wider, within the bound.
A program may use at most 64 MiB of HBM per device.

v0:
```python
import jax
import jax.numpy as jnp
from jax import lax
from jax.sharding import PartitionSpec as P


def shards(pair, cotangent, w_left, w_left_gate, w_right, w_right_gate):
    pair_f = pair.astype(jnp.float32)
    average = jnp.mean(pair_f, axis=-1, keepdims=True)
    centered_input = pair_f - average
    variance = jnp.mean(centered_input * centered_input, axis=-1, keepdims=True)
    inverse_scale = 1.0 / jnp.sqrt(variance + 1e-05)
    standardized_input = centered_input * inverse_scale
    normalized_input = standardized_input.astype(jnp.bfloat16)
    stacked = jnp.concatenate([w_left, w_left_gate, w_right, w_right_gate], axis=1)
    projected = jnp.einsum(
        "rcd,dh->hrc", normalized_input, stacked, preferred_element_type=jnp.float32
    )
    q_left, p_left, q_right, p_right = jnp.split(projected, 4, axis=0)
    s_left = jax.nn.sigmoid(p_left)
    s_right = jax.nn.sigmoid(p_right)
    left = (s_left * q_left).astype(jnp.bfloat16)
    right = (s_right * q_right).astype(jnp.bfloat16)
    g_chan, left_chan, right_chan = (
        lax.all_to_all(cotangent, "col", split_axis=0, concat_axis=2, tiled=True),
        lax.all_to_all(left, "col", split_axis=0, concat_axis=2, tiled=True),
        lax.all_to_all(right, "col", split_axis=0, concat_axis=2, tiled=True),
    )
    residues = g_chan.shape[2]
    col_block = g_chan
    d_left = jnp.einsum(
        "hij,hjk->hik",
        col_block,
        lax.all_gather(right_chan, "row", axis=1, tiled=True),
        preferred_element_type=jnp.float32,
    )
    col_block = g_chan
    summed = lax.psum_scatter(
        jnp.einsum("hij,hik->jhk", col_block, left_chan, preferred_element_type=jnp.float32),
        "row",
        scatter_dimension=0,
        tiled=True,
    )
    d_right = jnp.transpose(summed, (1, 0, 2))
    d_left_tile, d_right_tile = (
        lax.all_to_all(d_left.astype(jnp.bfloat16), "col", split_axis=2, concat_axis=0, tiled=True),
        lax.all_to_all(
            d_right.astype(jnp.bfloat16), "col", split_axis=2, concat_axis=0, tiled=True
        ),
    )
    grad_l = d_left_tile.astype(jnp.float32)
    grad_r = d_right_tile.astype(jnp.float32)
    e_left = grad_l * s_left
    f_left = grad_l * q_left * s_left * (1.0 - s_left)
    e_right = grad_r * s_right
    f_right = grad_r * q_right * s_right * (1.0 - s_right)
    grads = jnp.concatenate([e_left, f_left, e_right, f_right], axis=0).astype(jnp.bfloat16)
    local_weights = jnp.einsum(
        "rcd,hrc->dh", normalized_input, grads, preferred_element_type=jnp.float32
    )
    total_weights = lax.psum(local_weights, ("row", "col")) / residues
    normalized_gradient = jnp.einsum(
        "hrc,dh->rcd", grads, stacked, preferred_element_type=jnp.float32
    )
    gradient_mean = jnp.mean(normalized_gradient, axis=-1, keepdims=True)
    gradient_input_mean = jnp.mean(normalized_gradient * standardized_input, axis=-1, keepdims=True)
    pair_gradient = (
        (normalized_gradient - gradient_mean - standardized_input * gradient_input_mean)
        * inverse_scale
    ).astype(jnp.bfloat16)
    pieces_w = jnp.split(total_weights, 4, axis=1)
    return (pair_gradient, pieces_w[0], pieces_w[1], pieces_w[2], pieces_w[3])


def solution(mesh):
    in_specs = (P("row", "col", None), P(None, "row", "col"), P(), P(), P(), P())
    out_specs = (P("row", "col", None), P(), P(), P(), P())
    return jax.shard_map(shards, mesh=mesh, in_specs=in_specs, out_specs=out_specs, check_vma=False)
```

profile of v0, /device:TPU:2, one launch (start us, length us, event | category | flops | bytes accessed | tf_op | source)
XLA Modules:
  0.0 579.7 jit_solution(9537658770375944991)
XLA Ops:
  7.2 1.2 convert_reduce_fusion
  8.4 1.3 fusion.10
  9.8 0.8 copy.87
  10.6 0.8 copy.88
  11.4 0.8 copy.89
  12.3 0.8 copy.90
  13.1 1.4 fusion.18
  15.3 21.4 %all_to_all.72 = bf16[8,2,4096]{2,1,0:T(2,128)(2,1)S(1)} all-to-all(bf16[8,2,4096]{2,1,0:T(2,128)(2,1)S(1)} %reshape.47), channel_id=1, replica_groups=mesh['row'=32,'col'=8] {'col'}, dimensions={0} | all-to-all | bytes 262144 | tf_op jit(solution)/shard_map/all_to_all | solution.py:27
  37.1 0.9 all_to_all.56
  38.3 13.0 %all_to_all.73 = bf16[8,2,4096]{2,1,0:T(2,128)(2,1)S(1)} all-to-all(bf16[8,2,4096]{2,1,0:T(2,128)(2,1)S(1)} %reshape.45), channel_id=1, replica_groups=mesh['row'=32,'col'=8] {'col'}, dimensions={0} | all-to-all | bytes 262144 | tf_op jit(solution)/shard_map/all_to_all | solution.py:25
  51.9 43.9 %all-gather.2.cloned.1.call-done = bf16[8,512,512]{2,1,0:T(8,128)(2,1)} async-done(((bf16[8,16,512]{2,1,0:T(8,128)(2,1)}), bf16[8,512,512]{2,1,0:T(8,128)(2,1)}) %all-gather.2.cloned.1.call-update) | async-done | bytes 4194320 | tf_op jit(solution)/shard_map/all_gather | solution.py:34
  95.9 2.8 fusion
  98.7 0.8 copy.94
  99.5 1.1 reshape.49
  100.5 18.0 %all_to_all.74 = bf16[8,2,4096]{2,1,0:T(2,128)(2,1)S(1)} all-to-all(bf16[8,2,4096]{2,1,0:T(2,128)(2,1)S(1)} %reshape.49), channel_id=1, replica_groups=mesh['row'=32,'col'=8] {'col'}, dimensions={0} | all-to-all | bytes 262144 | tf_op jit(solution)/shard_map/all_to_all | solution.py:46
  118.6 0.7 reshape.50
  119.3 0.7 copy.95
  121.4 13.0 %all_to_all.75 = bf16[8,2,4096]{2,1,0:T(2,128)(2,1)S(1)} all-to-all(bf16[8,2,4096]{2,1,0:T(2,128)(2,1)S(1)} %reshape.51), channel_id=1, replica_groups=mesh['row'=32,'col'=8] {'col'}, dimensions={0} | all-to-all | bytes 262144 | tf_op jit(solution)/shard_map/all_to_all | solution.py:26
  135.1 4.5 convolution_bitcast_fusion
  139.6 10.4 %copy.101 = f32[512,8,512]{2,1,0:T(8,128)} copy(f32[512,8,512]{0,2,1:T(8,128)} %convolution_bitcast_fusion) | data formatting | bytes 16777216 | tf_op jit(solution)/shard_map/hij,hik->jhk/transpose | solution.py:39
  150.1 150.5 %reduce-scatter.2.cloned.1.call-done = f32[16,8,512]{2,1,0:T(8,128)} async-done(((f32[512,8,512]{2,1,0:T(8,128)}), f32[16,8,512]{2,1,0:T(8,128)}) %reduce-scatter.2.cloned.1.call-update) | async-done | bytes 262160 | tf_op jit(solution)/shard_map/reduce_scatter | solution.py:38
  300.5 1.0 convert_bitcast_fusion
  301.5 0.8 copy.102
  302.3 1.1 reshape.53
  303.4 16.3 %all_to_all.76 = bf16[8,2,4096]{2,1,0:T(2,128)(2,1)S(1)} all-to-all(bf16[8,2,4096]{2,1,0:T(2,128)(2,1)S(1)} %reshape.53), channel_id=1, replica_groups=mesh['row'=32,'col'=8] {'col'}, dimensions={0} | all-to-all | bytes 262144 | tf_op jit(solution)/shard_map/all_to_all | solution.py:47
  320.4 0.7 copy.103
  322.0 1.5 convolution_bitcast_fusion.1
  323.5 1.0 fusion.21
  324.5 1.3 fusion.9
  325.9 243.5 %all-reduce.2.cloned.1.call-done = f32[128,256]{1,0:T(8,128)} async-done(((f32[128,256]{1,0:T(8,128)}), f32[128,256]{1,0:T(8,128)}) %all-reduce.2.cloned.1.call-update) | async-done | bytes 131088 | tf_op jit(solution)/shard_map/psum | solution.py:61
  569.4 0.9 broadcast_multiply_fusion
  570.4 0.7 copy.110
  (40 shorter events, 7.8 us)
Async XLA Ops:
  7.2 30.9 %copy-start.1 = (bf16[64,16,64]{2,1,0:T(8,128)(2,1)S(1)}, bf16[64,16,64]{2,1,0:T(8,128)(2,1)}, u32[]{:S(2)}) copy-start(bf16[64,16,64]{2,1,0:T(8,128)(2,1)} %param.7) | copy-start | bytes 393220
  7.2 88.7 %all-gather.2.cloned.1.call-start = ((), (), s32[]{:S(2)}) async-start(), calls=%async_computation.6 | async-start | bytes 4325376 | tf_op jit(solution)/shard_map/all_gather | solution.py:34
  38.0 262.5 %reduce-scatter.2.cloned.1.call-start = ((), (), s32[]{:S(2)}) async-start(), calls=%async_computation.7 | async-start | bytes 8650752 | tf_op jit(solution)/shard_map/reduce_scatter | solution.py:38
  150.0 419.4 %all-reduce.2.cloned.1.call-start = ((), (), s32[]{:S(2)}) async-start(), calls=%async_computation.8 | async-start | bytes 262144 | tf_op jit(solution)/shard_map/psum | solution.py:61
  302.3 19.7 %copy-start = (bf16[16,64,128]{2,1,0:T(8,128)(2,1)S(1)}, bf16[16,64,128]{2,1,0:T(8,128)(2,1)}, u32[]{:S(2)}) copy-start(bf16[16,64,128]{2,1,0:T(8,128)(2,1)} %param.6) | copy-start | bytes 786436
Sparse Core Ops, SparseCore 0:
  38.1 57.7 all-gather.1
  150.1 150.3 reduce-scatter.1
  324.7 244.7 all-reduce.1
where the time goes:
time: 581 us; the launch traced here: 580 us
  waiting for transfers between devices  438 us (75%)
  blocking collectives  81.8 us (14%)
  local copies, waits for them, and re-layouts  27.9 us (5%)
  between operations  14 us (2%)
  matrix products  11.3 us (2%)
  other arithmetic  6.66 us (1%)
    psum x1, waiting for transfers between devices, shards(): total_weights = lax.psum(local_weights, ('row', 'col')) / residues  244 us
    reduce_scatter x1, waiting for transfers between devices, shards(): lax.psum_scatter(jnp.einsum('hij,hik->jhk', col_block, left_chan, preferr...  150 us
    all_gather x1, waiting for transfers between devices, shards(): lax.all_gather(right_chan, 'row', axis=1, tiled=True)  43.9 us
    all_to_all x1, blocking collectives, shards(): lax.all_to_all(right, 'col', split_axis=0, concat_axis=2, tiled=True)  21.4 us
    all_to_all x1, blocking collectives, shards(): lax.all_to_all(d_left.astype(jnp.bfloat16), 'col', split_axis=2, concat_a...  18 us
    all_to_all x1, blocking collectives, shards(): lax.all_to_all(d_right.astype(jnp.bfloat16), 'col', split_axis=2, concat_...  16.3 us
    all_to_all x1, blocking collectives, shards(): lax.all_to_all(left, 'col', split_axis=0, concat_axis=2, tiled=True)  13 us
    all_to_all x1, blocking collectives, shards(): lax.all_to_all(cotangent, 'col', split_axis=0, concat_axis=2, tiled=True)  13 us
  transfers between devices with their start and end apart: 3, of which 3 were waited for; matrix products, arithmetic and copies ran while one was open for 0% of the time, Pallas kernels for 0%

commit v1 on v0

--- a/solution.py
+++ b/solution.py
@@ -31,7 +31,9 @@
     d_left = jnp.einsum(
         "hij,hjk->hik",
         col_block,
-        lax.all_gather(right_chan, "row", axis=1, tiled=True),
+        jnp.concatenate(
+            lax.all_to_all(jnp.stack([right_chan] * lax.axis_size("row")), "row", 0, 0), axis=1
+        ),
         preferred_element_type=jnp.float32,
     )
     col_block = g_chan

time: 581 us -> 633 us (1.090)
  waiting for transfers between devices: 438 us -> 505 us
  blocking collectives: 81.8 us -> 42.1 us
  starting transfers between devices: 0.12 us -> 21.1 us
    all_to_all x0 -> x3, waiting for transfers between devices: none -> 112 us  [the longest x1 92.7 us: shards(): lax.all_to_all(jnp.stack([right_chan] * lax.axis_size('row')), 'row', 0, 0)]
    all_gather x1 -> x0, waiting for transfers between devices: 43.9 us -> none  [shards(): lax.all_gather(right_chan, 'row', axis=1, tiled=True)]
    all_to_all x2 -> x0, blocking collectives: 34.4 us -> none  [the longest x1 21.4 us: shards(): lax.all_to_all(right, 'col', split_axis=0, concat_axis=2, tiled=True)]
    all_to_all x0 -> x3, starting transfers between devices: none -> 20.9 us  [the longest x1 11.1 us: shards(): lax.all_to_all(right, 'col', split_axis=0, concat_axis=2, tiled=True)]
  transfers between devices with their start and end apart: 3 -> 5, of which waited for: 3 -> 5; matrix products, arithmetic and copies ran while one was open for 0% -> 1% of each run, Pallas kernels for 0% -> 0%
where the time goes in v1:
time: 633 us; the launch traced here: 632 us
  waiting for transfers between devices  505 us (80%)
  blocking collectives  42.1 us (7%)
  local copies, waits for them, and re-layouts  33.7 us (5%)
  starting transfers between devices  21.1 us (3%)
  between operations  14.3 us (2%)
  matrix products  9.11 us (1%)
  other arithmetic  6.67 us (1%)
    psum x1, waiting for transfers between devices, shards(): total_weights = lax.psum(local_weights, ('row', 'col')) / residues  243 us
    reduce_scatter x1, waiting for transfers between devices, shards(): lax.psum_scatter(jnp.einsum('hij,hik->jhk', col_block, left_chan, preferr...  150 us
    all_to_all x1, waiting for transfers between devices, shards(): lax.all_to_all(jnp.stack([right_chan] * lax.axis_size('row')), 'row', 0, 0)  92.7 us
    all_to_all x1, blocking collectives, shards(): lax.all_to_all(d_right.astype(jnp.bfloat16), 'col', split_axis=2, concat_...  16 us
    all_to_all x1, blocking collectives, shards(): lax.all_to_all(left, 'col', split_axis=0, concat_axis=2, tiled=True)  13.1 us
    all_to_all x1, blocking collectives, shards(): lax.all_to_all(d_left.astype(jnp.bfloat16), 'col', split_axis=2, concat_a...  13 us
  transfers between devices with their start and end apart: 5, of which 5 were waited for; matrix products, arithmetic and copies ran while one was open for 1% of the time, Pallas kernels for 0%

profile of v1, /device:TPU:2, one launch (start us, length us, event | category | flops | bytes accessed | tf_op | source)
XLA Modules:
  0.0 632.1 jit_solution(1455483045885680434)
XLA Ops:
  7.2 1.2 convert_reduce_fusion
  8.4 1.3 fusion.10
  9.7 0.8 copy.88
  10.6 0.8 copy.89
  11.4 0.8 copy.90
  12.2 0.8 copy.91
  13.1 1.4 fusion.18
  15.0 0.9 reshape.58
  15.9 11.1 %all-to-all-start = ((bf16[8,2,4096]{2,1,0:T(2,128)(2,1)}), bf16[8,2,4096]{2,1,0:T(2,128)(2,1)S(1)}, u32[]{:S(2)}, u32[]{:S(2)}) async-start(bf16[8,2,4096]{2,1,0:T(2,128)(2,1)} %reshape.58), calls=%async_computation | async-start | bytes 262144 | tf_op jit(solution)/shard_map/all_to_all | solution.py:27
  27.0 0.9 reshape.56
  27.9 9.6 %all-to-all-done = bf16[8,2,4096]{2,1,0:T(2,128)(2,1)S(1)} async-done(((bf16[8,2,4096]{2,1,0:T(2,128)(2,1)}), bf16[8,2,4096]{2,1,0:T(2,128)(2,1)S(1)}, u32[]{:S(2)}, u32[]{:S(2)}) %all-to-all-start) | async-done | bytes 131104 | tf_op jit(solution)/shard_map/all_to_all | solution.py:27
  37.5 3.4 all-to-all-start.2
  41.5 9.8 %all-to-all-done.2 = bf16[8,2,4096]{2,1,0:T(2,128)(2,1)S(1)} async-done(((bf16[8,2,4096]{2,1,0:T(2,128)(2,1)}), bf16[8,2,4096]{2,1,0:T(2,128)(2,1)S(1)}, u32[]{:S(2)}, u32[]{:S(2)}) %all-to-all-start.2) | async-done | bytes 131104 | tf_op jit(solution)/shard_map/all_to_all | solution.py:25
  51.3 2.5 stack.5
  53.8 6.4 %all-to-all-start.1 = ((bf16[32,8,16,512]{3,2,1,0:T(8,128)(2,1)}), bf16[32,8,16,512]{3,2,1,0:T(8,128)(2,1)}, u32[]{:S(2)}, u32[]{:S(2)}) async-start(bf16[32,8,16,512]{3,2,1,0:T(8,128)(2,1)} %stack.5), calls=%async_computation.1 | async-start | bytes 8388608 | tf_op jit(solution)/shard_map/all_to_all | solution.py:35
  60.9 92.7 %all-to-all-done.1 = bf16[32,8,16,512]{3,2,1,0:T(8,128)(2,1)} async-done(((bf16[32,8,16,512]{3,2,1,0:T(8,128)(2,1)}), bf16[32,8,16,512]{3,2,1,0:T(8,128)(2,1)}, u32[]{:S(2)}, u32[]{:S(2)}) %all-to-all-start.1) | async-done | bytes 4194336 | tf_op jit(solution)/shard_map/all_to_all | solution.py:35
  153.6 2.7 copy.94
  157.7 1.1 reshape.60
  158.7 13.0 %all_to_all.74 = bf16[8,2,4096]{2,1,0:T(2,128)(2,1)S(1)} all-to-all(bf16[8,2,4096]{2,1,0:T(2,128)(2,1)S(1)} %reshape.60), channel_id=1, replica_groups=mesh['row'=32,'col'=8] {'col'}, dimensions={0} | all-to-all | bytes 262144 | tf_op jit(solution)/shard_map/all_to_all | solution.py:48
  174.6 13.1 %all_to_all.75 = bf16[8,2,4096]{2,1,0:T(2,128)(2,1)S(1)} all-to-all(bf16[8,2,4096]{2,1,0:T(2,128)(2,1)S(1)} %reshape.62), channel_id=1, replica_groups=mesh['row'=32,'col'=8] {'col'}, dimensions={0} | all-to-all | bytes 262144 | tf_op jit(solution)/shard_map/all_to_all | solution.py:26
  188.3 4.5 convolution_bitcast_fusion
  192.8 10.4 %copy.103 = f32[512,8,512]{2,1,0:T(8,128)} copy(f32[512,8,512]{0,2,1:T(8,128)} %convolution_bitcast_fusion) | data formatting | bytes 16777216 | tf_op jit(solution)/shard_map/hij,hik->jhk/transpose | solution.py:41
  203.5 149.8 %reduce-scatter.2.cloned.1.call-done = f32[16,8,512]{2,1,0:T(8,128)} async-done(((f32[512,8,512]{2,1,0:T(8,128)}), f32[16,8,512]{2,1,0:T(8,128)}) %reduce-scatter.2.cloned.1.call-update) | async-done | bytes 262160 | tf_op jit(solution)/shard_map/reduce_scatter | solution.py:40
  353.3 1.0 convert_bitcast_fusion
  354.3 0.8 copy.104
  355.1 1.1 reshape.64
  356.2 16.0 %all_to_all.76 = bf16[8,2,4096]{2,1,0:T(2,128)(2,1)S(1)} all-to-all(bf16[8,2,4096]{2,1,0:T(2,128)(2,1)S(1)} %reshape.64), channel_id=1, replica_groups=mesh['row'=32,'col'=8] {'col'}, dimensions={0} | all-to-all | bytes 262144 | tf_op jit(solution)/shard_map/all_to_all | solution.py:49
  374.4 1.5 convolution_bitcast_fusion.1
  375.9 1.0 fusion.21
  377.0 1.3 fusion.9
  378.3 243.2 %all-reduce.2.cloned.1.call-done = f32[128,256]{1,0:T(8,128)} async-done(((f32[128,256]{1,0:T(8,128)}), f32[128,256]{1,0:T(8,128)}) %all-reduce.2.cloned.1.call-update) | async-done | bytes 131088 | tf_op jit(solution)/shard_map/psum | solution.py:63
  621.5 0.9 broadcast_multiply_fusion
  (43 shorter events, 11.9 us)
Async XLA Ops:
  7.2 19.8 %copy-start.1 = (bf16[64,16,64]{2,1,0:T(8,128)(2,1)S(1)}, bf16[64,16,64]{2,1,0:T(8,128)(2,1)}, u32[]{:S(2)}) copy-start(bf16[64,16,64]{2,1,0:T(8,128)(2,1)} %param.7) | copy-start | bytes 393220
  15.9 21.6 %all-to-all-start = ((bf16[8,2,4096]{2,1,0:T(2,128)(2,1)}), bf16[8,2,4096]{2,1,0:T(2,128)(2,1)S(1)}, u32[]{:S(2)}, u32[]{:S(2)}) async-start(bf16[8,2,4096]{2,1,0:T(2,128)(2,1)} %reshape.58), calls=%async_computation | async-start | bytes 262144 | tf_op jit(solution)/shard_map/all_to_all | solution.py:27
  37.5 13.8 %all-to-all-start.2 = ((bf16[8,2,4096]{2,1,0:T(2,128)(2,1)}), bf16[8,2,4096]{2,1,0:T(2,128)(2,1)S(1)}, u32[]{:S(2)}, u32[]{:S(2)}) async-start(bf16[8,2,4096]{2,1,0:T(2,128)(2,1)} %reshape.56), calls=%async_computation.2 | async-start | bytes 262144 | tf_op jit(solution)/shard_map/all_to_all | solution.py:25
  53.8 99.8 %all-to-all-start.1 = ((bf16[32,8,16,512]{3,2,1,0:T(8,128)(2,1)}), bf16[32,8,16,512]{3,2,1,0:T(8,128)(2,1)}, u32[]{:S(2)}, u32[]{:S(2)}) async-start(bf16[32,8,16,512]{3,2,1,0:T(8,128)(2,1)} %stack.5), calls=%async_computation.1 | async-start | bytes 8388608 | tf_op jit(solution)/shard_map/all_to_all | solution.py:35
  60.2 293.1 %reduce-scatter.2.cloned.1.call-start = ((), (), s32[]{:S(2)}) async-start(), calls=%async_computation.7 | async-start | bytes 8650752 | tf_op jit(solution)/shard_map/reduce_scatter | solution.py:40
  203.3 418.2 %all-reduce.2.cloned.1.call-start = ((), (), s32[]{:S(2)}) async-start(), calls=%async_computation.8 | async-start | bytes 262144 | tf_op jit(solution)/shard_map/psum | solution.py:63
  355.1 19.3 %copy-start = (bf16[16,64,128]{2,1,0:T(8,128)(2,1)S(1)}, bf16[16,64,128]{2,1,0:T(8,128)(2,1)}, u32[]{:S(2)}) copy-start(bf16[16,64,128]{2,1,0:T(8,128)(2,1)} %param.6) | copy-start | bytes 786436
Sparse Core Ops, SparseCore 0:
  203.4 149.8 reduce-scatter.1
  377.1 244.3 all-reduce.1
